TPU v7x, 256 devices: a whole 4x4x8 slice. The times are simulated.
256 devices in a mesh: height: 8 (over z_hi, core), plane: 32 (over z_lo, y, x).
Axes of the slice: x: 4, y: 4, z: 8 (z_hi: 4, z_lo: 2; z = z_hi * 2 + z_lo), core: 2. Of those that a mesh axis runs over, the one named last changes fastest.
Arguments:
- cotangent: float32 [128, 256, 128], P('height', 'plane'), may hold values from -36 to 36
- conductivity: float32 [16, 32, 16], P('height', 'plane'), may hold values from 0.2 to 5
- capacity: float32 [16, 32, 16], P('height', 'plane'), may hold values from 0.5 to 2
- sources: int32 [2, 128], replicated, may hold values from 0 to 8191
Outputs:
- adjoint_second: float32 [128, 256, 128], P('height', 'plane')
- adjoint_first: float32 [128, 256, 128], P('height', 'plane')
- source_grad: float32 [2, 128], replicated
Inputs may be any that keep to these rules, and one draw needn't show every extreme that they name: `sources`: element numbers; element (ez, ex, ey) has number (ez * 32 + ex) * 16 + ey, and a number may repeat.
All inputs are finite; a program needn't handle non-finite values.
Results may differ from a plain program's by a relative error of at most 0.0001.
Values sent between devices are 32-bit elements; how exact they have to be, the bound alone decides.
A program may use at most 64 MiB of HBM per device.

v0:
```python
import jax
import jax.numpy as jnp
import numpy as np
from jax import lax
from jax.sharding import Mesh
from jax.sharding import PartitionSpec as P

ITERS = 3
HEIGHT = ("height_0", "height_1")
PLANE = ("plane_0", "plane_1", "plane_2")
HEIGHT_PLANE = ("height_0", "height_1", "plane_0", "plane_1", "plane_2")
precise = lax.Precision.HIGHEST
INV_STEP = 20.0


def with_halo(block, sides, width):
    for axis, dim in sides:
        count = lax.axis_size(axis)
        forward = [(i, i + 1) for i in range(count - 1)]
        backward = [(target, source) for source, target in forward]
        low = lax.ppermute(
            lax.slice_in_dim(block, block.shape[dim] - width, None, axis=dim), axis, forward
        )
        high = lax.ppermute(lax.slice_in_dim(block, 0, width, axis=dim), axis, backward)
        block = jnp.concatenate([low, block, high], axis=dim)
    return block


def by_axis(value, axes):
    for axis in axes:
        value = lax.psum(value, axis)
    return value


def gll_tables():
    points = np.array(
        [
            -1.0,
            -0.8717401485096066,
            -0.5917001814331423,
            -0.2092992179024789,
            0.2092992179024789,
            0.5917001814331423,
            0.8717401485096066,
            1.0,
        ]
    )
    weights = np.array(
        [
            1.0 / 28.0,
            0.2107042271435061,
            0.3411226924835044,
            0.4124587946587038,
            0.4124587946587038,
            0.3411226924835044,
            0.2107042271435061,
            1.0 / 28.0,
        ]
    )
    product = np.array(
        [
            np.prod([points[column] - points[others] for others in range(8) if others != column])
            for column in range(8)
        ]
    )
    derivative = np.zeros((8, 8))
    for row_idx in range(8):
        for col_idx in range(8):
            if row_idx != col_idx:
                derivative[row_idx, col_idx] = product[row_idx] / (
                    product[col_idx] * (points[row_idx] - points[col_idx])
                )
        derivative[row_idx, row_idx] = -np.sum(derivative[row_idx])
    stiff_diag = np.sum(derivative**2 * weights[:, None], axis=0)
    return (derivative, weights, stiff_diag)


def pair_sum(values, dim_index):
    shape = values.shape
    count = shape[dim_index] // 8
    split = values.reshape(shape[:dim_index] + (count, 8) + shape[dim_index + 1 :])
    slot_axis = dim_index + 1
    slot_first = lax.slice_in_dim(split, 0, 1, axis=slot_axis)
    slot_last = lax.slice_in_dim(split, 7, 8, axis=slot_axis)
    middle = lax.slice_in_dim(split, 1, 7, axis=slot_axis)
    joined = lax.slice_in_dim(slot_last, 0, count - 1, axis=dim_index) + lax.slice_in_dim(
        slot_first, 1, count, axis=dim_index
    )
    new_last = jnp.concatenate(
        [joined, lax.slice_in_dim(slot_last, count - 1, count, axis=dim_index)], axis=dim_index
    )
    new_first = jnp.concatenate(
        [lax.slice_in_dim(slot_first, 0, 1, axis=dim_index), joined], axis=dim_index
    )
    rebuilt = jnp.concatenate([new_first, middle, new_last], axis=slot_axis)
    return rebuilt.reshape(shape)


def add_edges(values, lower, upper, dim_index):
    extent = values.shape[dim_index]
    first = lax.slice_in_dim(values, 0, 1, axis=dim_index) + jnp.expand_dims(lower, dim_index)
    inside = lax.slice_in_dim(values, 1, extent - 1, axis=dim_index)
    last = lax.slice_in_dim(values, extent - 1, extent, axis=dim_index) + jnp.expand_dims(
        upper, dim_index
    )
    return jnp.concatenate([first, inside, last], axis=dim_index)


def multiplicity(local_count, offset, extent):
    position = offset + jnp.arange(local_count, dtype=jnp.int32)
    ending = ((position % 8 == 7) & (position < extent - 1)).astype(jnp.float32)
    opening = ((position % 8 == 0) & (position > 0)).astype(jnp.float32)
    return 1.0 + ending + opening


def per_device(cotangent, conductivity, capacity, sources):
    derivative, weights, stiff_diag = gll_tables()
    depth_nodes, width_nodes, span_nodes = cotangent.shape
    elem_depth, elem_width, elem_span = (depth_nodes // 8, width_nodes // 8, span_nodes // 8)
    diff = jnp.asarray(derivative, jnp.float32)
    weight_depth = jnp.asarray(np.tile(weights, elem_depth), jnp.float32)
    weight_width = jnp.asarray(np.tile(weights, elem_width), jnp.float32)
    weight_span = jnp.asarray(np.tile(weights, elem_span), jnp.float32)
    stiff_depth = jnp.asarray(np.tile(stiff_diag, elem_depth), jnp.float32)
    stiff_width = jnp.asarray(np.tile(stiff_diag, elem_width), jnp.float32)
    stiff_span = jnp.asarray(np.tile(stiff_diag, elem_span), jnp.float32)
    kappa_nodes = jnp.repeat(jnp.repeat(jnp.repeat(conductivity, 8, axis=0), 8, axis=1), 8, axis=2)
    cap_nodes = jnp.repeat(jnp.repeat(jnp.repeat(capacity, 8, axis=0), 8, axis=1), 8, axis=2)
    omega_nodes = (
        weight_depth[:, None, None] * weight_width[None, :, None] * weight_span[None, None, :]
    )
    mass_local = INV_STEP * cap_nodes * omega_nodes
    kappa_weight = kappa_nodes * omega_nodes
    diag_local = mass_local + kappa_nodes * (
        stiff_depth[:, None, None] * weight_width[None, :, None] * weight_span[None, None, :]
        + weight_depth[:, None, None] * stiff_width[None, :, None] * weight_span[None, None, :]
        + weight_depth[:, None, None] * weight_width[None, :, None] * stiff_span[None, None, :]
    )
    height_pos = lax.axis_index(HEIGHT)
    plane_pos = lax.axis_index(PLANE)
    copies_depth = multiplicity(
        depth_nodes, height_pos * depth_nodes, depth_nodes * lax.axis_size(HEIGHT)
    )
    copies_width = multiplicity(
        width_nodes, plane_pos * width_nodes, width_nodes * lax.axis_size(PLANE)
    )
    copies_span = multiplicity(span_nodes, 0, span_nodes)
    share_weight = 1.0 / (
        copies_depth[:, None, None] * copies_width[None, :, None] * copies_span[None, None, :]
    )
    shape_depth = (elem_depth, 8, width_nodes, span_nodes)
    shape_width = (depth_nodes, elem_width, 8, span_nodes)
    shape_span = (depth_nodes, width_nodes, elem_span, 8)
    full_shape = cotangent.shape

    def stiffness(values):
        grad_depth = jnp.einsum(
            "ab,ebxy->eaxy", diff, values.reshape(shape_depth), precision=precise
        ).reshape(full_shape)
        grad_width = jnp.einsum(
            "ab,zeby->zeay", diff, values.reshape(shape_width), precision=precise
        ).reshape(full_shape)
        grad_span = jnp.einsum(
            "ab,zxeb->zxea", diff, values.reshape(shape_span), precision=precise
        ).reshape(full_shape)
        back_depth = jnp.einsum(
            "ab,eaxy->ebxy",
            diff,
            (kappa_weight * grad_depth).reshape(shape_depth),
            precision=precise,
        ).reshape(full_shape)
        back_width = jnp.einsum(
            "ab,zeay->zeby",
            diff,
            (kappa_weight * grad_width).reshape(shape_width),
            precision=precise,
        ).reshape(full_shape)
        back_span = jnp.einsum(
            "ab,zxea->zxeb", diff, (kappa_weight * grad_span).reshape(shape_span), precision=precise
        ).reshape(full_shape)
        return mass_local * values + (back_depth + back_width + back_span)

    def assemble(contrib):
        summed = pair_sum(contrib, 1)
        face_pair = jnp.stack([summed[:, 0], summed[:, -1]])
        received = with_halo(face_pair, ((PLANE, 0),), 1)
        summed = add_edges(summed, received[0], received[3], 1)
        summed = pair_sum(summed, 2)
        summed = pair_sum(summed, 0)
        face_pair = jnp.stack([summed[0], summed[-1]])
        received = with_halo(face_pair, ((HEIGHT, 0),), 1)
        summed = add_edges(summed, received[0], received[3], 0)
        return summed

    diag_total = assemble(diag_local)

    def inner_sum(left_values, right_values):
        return jnp.sum(left_values * right_values * share_weight)

    def paired_sums(residual, precond, applied):
        return (
            by_axis(inner_sum(residual, precond), HEIGHT_PLANE),
            by_axis(inner_sum(precond, applied), HEIGHT_PLANE),
        )

    def adjoint_solve(source_term):
        iterate = jnp.zeros_like(source_term)
        residual = source_term
        precond = residual / diag_total
        applied = assemble(stiffness(precond))
        rho_now, curvature_now = paired_sums(residual, precond, applied)
        step_len = rho_now / curvature_now
        direction, applied_dir = (precond, applied)
        for sweep_idx in range(ITERS):
            iterate = iterate + step_len * direction
            residual = residual - step_len * applied_dir
            if sweep_idx + 1 < ITERS:
                precond = residual / diag_total
                applied = assemble(stiffness(precond))
                rho_next, curvature_now = paired_sums(residual, precond, applied)
                beta_now = rho_next / rho_now
                step_len = rho_next / (curvature_now - beta_now * rho_next / step_len)
                direction = precond + beta_now * direction
                applied_dir = applied + beta_now * applied_dir
                rho_now = rho_next
        return iterate

    adjoint_second = adjoint_solve(assemble(mass_local * cotangent))
    adjoint_first = adjoint_solve(assemble(mass_local * adjoint_second))

    def element_sums(values):
        return (
            (mass_local * values)
            .reshape(elem_depth, 8, elem_width, 8, elem_span, 8)
            .sum(axis=(1, 3, 5))
            .reshape(-1)
        )

    depth_ids = height_pos * elem_depth + jnp.arange(elem_depth, dtype=jnp.int32)
    width_ids = plane_pos * elem_width + jnp.arange(elem_width, dtype=jnp.int32)
    span_ids = jnp.arange(elem_span, dtype=jnp.int32)
    global_ids = (
        (depth_ids[:, None, None] * (elem_width * lax.axis_size(PLANE)) + width_ids[None, :, None])
        * elem_span
        + span_ids[None, None, :]
    ).reshape(-1)
    matches = (sources[:, :, None] == global_ids[None, None, :]).astype(jnp.float32)
    stacked = jnp.stack([element_sums(adjoint_first), element_sums(adjoint_second)])
    local_grad = jnp.sum(matches * stacked[:, None, :], axis=2) / (8.0 * INV_STEP)
    source_grad = by_axis(local_grad, HEIGHT_PLANE)
    return (adjoint_second, adjoint_first, source_grad)


def solution(mesh):
    torus = Mesh(
        mesh.devices.reshape(4, 2, 2, 4, 4),
        ("height_0", "height_1", "plane_0", "plane_1", "plane_2"),
    )
    in_specs = (P(HEIGHT, PLANE, None), P(HEIGHT, PLANE, None), P(HEIGHT, PLANE, None), P())
    out_specs = (P(HEIGHT, PLANE, None), P(HEIGHT, PLANE, None), P())
    return jax.shard_map(
        per_device, mesh=torus, in_specs=in_specs, out_specs=out_specs, check_vma=False
    )
```

profile of v0, /device:TPU:32, one launch (start us, length us, event | category | flops | bytes accessed | tf_op | source)
XLA Modules:
  0.0 619.1 jit_solution(5924039357253997425)
XLA Ops:
  3.8 6.7 %collective-permute-start.5 = (f32[1,16,128]{2,1,0:T(8,128)S(1)}, f32[1,16,128]{2,1,0:T(8,128)S(1)}, u32[]{:S(2)}, u32[]{:S(2)}) collective-permute-start(f32[1,16,128]{2,1,0:T(8,128)S(1)} %bitcast.647), channel_id=1, source_target_pairs={{1,0},{2,1},{3,2},{4,3},{5,4},{6,5},{7,6},{8,7},{9,8},{10,9},{11,1... | collective-permute-start | bytes 24584 | tf_op jit(solution)/shard_map/ppermute | solution.py:24
  45.8 6.5 %collective-permute-start.2 = (f32[1,8,128]{2,1,0:T(8,128)S(1)}, f32[1,8,128]{2,1,0:T(8,128)S(1)}, u32[]{:S(2)}, u32[]{:S(2)}) collective-permute-start(f32[1,8,128]{2,1,0:T(8,128)S(1)} %get-tuple-element.211), channel_id=1, source_target_pairs={{0,32},{32,64},{64,96},{96,128},{128,160},{160,192},{192,224},{1,3... | collective-permute-start | bytes 12296 | tf_op jit(solution)/shard_map/ppermute | solution.py:21
  70.9 7.3 %collective-permute-done.8 = f32[1,16,128]{2,1,0:T(8,128)S(1)} collective-permute-done((f32[1,16,128]{2,1,0:T(8,128)S(1)}, f32[1,16,128]{2,1,0:T(8,128)S(1)}, u32[]{:S(2)}, u32[]{:S(2)}) %collective-permute-start.8) | collective-permute-done | bytes 8224 | tf_op jit(solution)/shard_map/ppermute | solution.py:21
  98.0 14.5 %all-reduce.17 = (f32[]{:T(128)}, f32[]{:T(128)}) all-reduce(f32[]{:T(128)} %get-tuple-element.14, f32[]{:T(128)} %get-tuple-element.13), channel_id=1, replica_groups=mesh['height_0'=4,'height_1'=2,'plane_0'=2,'plane_1'=4,'plane_2'=4] {'he..., use_global_device_ids=true, to_apply=%region_1.2 | all-reduce | flops 2 | bytes 16 | tf_op jit(solution)/shard_map/psum | solution.py:31
  117.5 5.6 all-reduce.23
  123.1 8.4 %all-reduce.11 = (f32[]{:T(128)}, f32[]{:T(128)}) all-reduce(f32[]{:T(128)} %get-tuple-element.61, f32[]{:T(128)} %get-tuple-element.62), channel_id=1, replica_groups=mesh['height_0'=4,'height_1'=2,'plane_0'=2,'plane_1'=4,'plane_2'=4] {'pl..., use_global_device_ids=true, to_apply=%region_4.5 | all-reduce | flops 2 | bytes 16 | tf_op jit(solution)/shard_map/psum | solution.py:31
  131.5 9.3 %all-reduce.5 = (f32[]{:T(128)}, f32[]{:T(128)}) all-reduce(f32[]{:T(128)} %get-tuple-element.37, f32[]{:T(128)} %get-tuple-element.38), channel_id=1, replica_groups=mesh['height_0'=4,'height_1'=2,'plane_0'=2,'plane_1'=4,'plane_2'=4] {'pl..., use_global_device_ids=true, to_apply=%region_5.6 | all-reduce | flops 2 | bytes 16 | tf_op jit(solution)/shard_map/psum | solution.py:31
  155.7 6.7 %collective-permute-done.12 = f32[1,16,128]{2,1,0:T(8,128)S(1)} collective-permute-done((f32[1,16,128]{2,1,0:T(8,128)S(1)}, f32[1,16,128]{2,1,0:T(8,128)S(1)}, u32[]{:S(2)}, u32[]{:S(2)}) %collective-permute-start.12) | collective-permute-done | bytes 8224 | tf_op jit(solution)/shard_map/ppermute | solution.py:21
  178.2 13.6 %all-reduce.16 = (f32[]{:T(128)}, f32[]{:T(128)}) all-reduce(f32[]{:T(128)} %get-tuple-element.12, f32[]{:T(128)} %get-tuple-element.11), channel_id=1, replica_groups=mesh['height_0'=4,'height_1'=2,'plane_0'=2,'plane_1'=4,'plane_2'=4] {'he..., use_global_device_ids=true, to_apply=%region_13.14 | all-reduce | flops 2 | bytes 16 | tf_op jit(solution)/shard_map/psum | solution.py:31
  201.4 8.4 %all-reduce.10 = (f32[]{:T(128)}, f32[]{:T(128)}) all-reduce(f32[]{:T(128)} %get-tuple-element.59, f32[]{:T(128)} %get-tuple-element.60), channel_id=1, replica_groups=mesh['height_0'=4,'height_1'=2,'plane_0'=2,'plane_1'=4,'plane_2'=4] {'pl..., use_global_device_ids=true, to_apply=%region_16.17 | all-reduce | flops 2 | bytes 16 | tf_op jit(solution)/shard_map/psum | solution.py:31
  209.8 9.9 %all-reduce.4 = (f32[]{:T(128)}, f32[]{:T(128)}) all-reduce(f32[]{:T(128)} %get-tuple-element.35, f32[]{:T(128)} %get-tuple-element.36), channel_id=1, replica_groups=mesh['height_0'=4,'height_1'=2,'plane_0'=2,'plane_1'=4,'plane_2'=4] {'pl..., use_global_device_ids=true, to_apply=%region_17.18 | all-reduce | flops 2 | bytes 16 | tf_op jit(solution)/shard_map/psum | solution.py:31
  238.0 6.9 %collective-permute-done.16 = f32[1,16,128]{2,1,0:T(8,128)S(1)} collective-permute-done((f32[1,16,128]{2,1,0:T(8,128)S(1)}, f32[1,16,128]{2,1,0:T(8,128)S(1)}, u32[]{:S(2)}, u32[]{:S(2)}) %collective-permute-start.16) | collective-permute-done | bytes 8224 | tf_op jit(solution)/shard_map/ppermute | solution.py:21
  260.7 13.7 %all-reduce.15 = (f32[]{:T(128)}, f32[]{:T(128)}) all-reduce(f32[]{:T(128)} %get-tuple-element.10, f32[]{:T(128)} %get-tuple-element.9), channel_id=1, replica_groups=mesh['height_0'=4,'height_1'=2,'plane_0'=2,'plane_1'=4,'plane_2'=4] {'he..., use_global_device_ids=true, to_apply=%region_25.26 | all-reduce | flops 2 | bytes 16 | tf_op jit(solution)/shard_map/psum | solution.py:31
  283.9 8.3 %all-reduce.9 = (f32[]{:T(128)}, f32[]{:T(128)}) all-reduce(f32[]{:T(128)} %get-tuple-element.57, f32[]{:T(128)} %get-tuple-element.58), channel_id=1, replica_groups=mesh['height_0'=4,'height_1'=2,'plane_0'=2,'plane_1'=4,'plane_2'=4] {'pl..., use_global_device_ids=true, to_apply=%region_28.29 | all-reduce | flops 2 | bytes 16 | tf_op jit(solution)/shard_map/psum | solution.py:31
  292.2 9.3 %all-reduce.3 = (f32[]{:T(128)}, f32[]{:T(128)}) all-reduce(f32[]{:T(128)} %get-tuple-element.33, f32[]{:T(128)} %get-tuple-element.34), channel_id=1, replica_groups=mesh['height_0'=4,'height_1'=2,'plane_0'=2,'plane_1'=4,'plane_2'=4] {'pl..., use_global_device_ids=true, to_apply=%region_29.30 | all-reduce | flops 2 | bytes 16 | tf_op jit(solution)/shard_map/psum | solution.py:31
  313.1 7.6 %collective-permute-done.20 = f32[1,16,128]{2,1,0:T(8,128)S(1)} collective-permute-done((f32[1,16,128]{2,1,0:T(8,128)S(1)}, f32[1,16,128]{2,1,0:T(8,128)S(1)}, u32[]{:S(2)}, u32[]{:S(2)}) %collective-permute-start.20) | collective-permute-done | bytes 8224 | tf_op jit(solution)/shard_map/ppermute | solution.py:21
  348.2 7.6 %collective-permute-done.24 = f32[1,16,128]{2,1,0:T(8,128)S(1)} collective-permute-done((f32[1,16,128]{2,1,0:T(8,128)S(1)}, f32[1,16,128]{2,1,0:T(8,128)S(1)}, u32[]{:S(2)}, u32[]{:S(2)}) %collective-permute-start.24) | collective-permute-done | bytes 8224 | tf_op jit(solution)/shard_map/ppermute | solution.py:21
  373.8 13.8 %all-reduce.14 = (f32[]{:T(128)}, f32[]{:T(128)}) all-reduce(f32[]{:T(128)} %get-tuple-element.8, f32[]{:T(128)} %get-tuple-element.7), channel_id=1, replica_groups=mesh['height_0'=4,'height_1'=2,'plane_0'=2,'plane_1'=4,'plane_2'=4] {'he..., use_global_device_ids=true, to_apply=%region_37.38 | all-reduce | flops 2 | bytes 16 | tf_op jit(solution)/shard_map/psum | solution.py:31
  392.6 5.6 all-reduce.20
  398.2 8.4 %all-reduce.8 = (f32[]{:T(128)}, f32[]{:T(128)}) all-reduce(f32[]{:T(128)} %get-tuple-element.55, f32[]{:T(128)} %get-tuple-element.56), channel_id=1, replica_groups=mesh['height_0'=4,'height_1'=2,'plane_0'=2,'plane_1'=4,'plane_2'=4] {'pl..., use_global_device_ids=true, to_apply=%region_40.41 | all-reduce | flops 2 | bytes 16 | tf_op jit(solution)/shard_map/psum | solution.py:31
  406.7 8.4 %all-reduce.2 = (f32[]{:T(128)}, f32[]{:T(128)}) all-reduce(f32[]{:T(128)} %get-tuple-element.31, f32[]{:T(128)} %get-tuple-element.32), channel_id=1, replica_groups=mesh['height_0'=4,'height_1'=2,'plane_0'=2,'plane_1'=4,'plane_2'=4] {'pl..., use_global_device_ids=true, to_apply=%region_41.42 | all-reduce | flops 2 | bytes 16 | tf_op jit(solution)/shard_map/psum | solution.py:31
  431.5 5.7 collective-permute-done.28
  453.1 13.6 %all-reduce.13 = (f32[]{:T(128)}, f32[]{:T(128)}) all-reduce(f32[]{:T(128)} %get-tuple-element.6, f32[]{:T(128)} %get-tuple-element.5), channel_id=1, replica_groups=mesh['height_0'=4,'height_1'=2,'plane_0'=2,'plane_1'=4,'plane_2'=4] {'he..., use_global_device_ids=true, to_apply=%region_49.50 | all-reduce | flops 2 | bytes 16 | tf_op jit(solution)/shard_map/psum | solution.py:31
  476.2 8.4 %all-reduce.7 = (f32[]{:T(128)}, f32[]{:T(128)}) all-reduce(f32[]{:T(128)} %get-tuple-element.53, f32[]{:T(128)} %get-tuple-element.54), channel_id=1, replica_groups=mesh['height_0'=4,'height_1'=2,'plane_0'=2,'plane_1'=4,'plane_2'=4] {'pl..., use_global_device_ids=true, to_apply=%region_52.53 | all-reduce | flops 2 | bytes 16 | tf_op jit(solution)/shard_map/psum | solution.py:31
  484.6 9.5 %all-reduce.1 = (f32[]{:T(128)}, f32[]{:T(128)}) all-reduce(f32[]{:T(128)} %get-tuple-element.29, f32[]{:T(128)} %get-tuple-element.30), channel_id=1, replica_groups=mesh['height_0'=4,'height_1'=2,'plane_0'=2,'plane_1'=4,'plane_2'=4] {'pl..., use_global_device_ids=true, to_apply=%region_53.54 | all-reduce | flops 2 | bytes 16 | tf_op jit(solution)/shard_map/psum | solution.py:31
  512.2 6.6 %collective-permute-done.32 = f32[1,16,128]{2,1,0:T(8,128)S(1)} collective-permute-done((f32[1,16,128]{2,1,0:T(8,128)S(1)}, f32[1,16,128]{2,1,0:T(8,128)S(1)}, u32[]{:S(2)}, u32[]{:S(2)}) %collective-permute-start.32) | collective-permute-done | bytes 8224 | tf_op jit(solution)/shard_map/ppermute | solution.py:21
  534.5 13.6 %all-reduce.12 = (f32[]{:T(128)}, f32[]{:T(128)}) all-reduce(f32[]{:T(128)} %get-tuple-element.4, f32[]{:T(128)} %get-tuple-element.3), channel_id=1, replica_groups=mesh['height_0'=4,'height_1'=2,'plane_0'=2,'plane_1'=4,'plane_2'=4] {'he..., use_global_device_ids=true, to_apply=%region_61.62 | all-reduce | flops 2 | bytes 16 | tf_op jit(solution)/shard_map/psum | solution.py:31
  557.5 8.3 %all-reduce.6 = (f32[]{:T(128)}, f32[]{:T(128)}) all-reduce(f32[]{:T(128)} %get-tuple-element.51, f32[]{:T(128)} %get-tuple-element.52), channel_id=1, replica_groups=mesh['height_0'=4,'height_1'=2,'plane_0'=2,'plane_1'=4,'plane_2'=4] {'pl..., use_global_device_ids=true, to_apply=%region_64.65 | all-reduce | flops 2 | bytes 16 | tf_op jit(solution)/shard_map/psum | solution.py:31
  565.9 9.2 %all-reduce = (f32[]{:T(128)}, f32[]{:T(128)}) all-reduce(f32[]{:T(128)} %get-tuple-element.27, f32[]{:T(128)} %get-tuple-element.28), channel_id=1, replica_groups=mesh['height_0'=4,'height_1'=2,'plane_0'=2,'plane_1'=4,'plane_2'=4] {'pl..., use_global_device_ids=true, to_apply=%region_65.66 | all-reduce | flops 2 | bytes 16 | tf_op jit(solution)/shard_map/psum | solution.py:31
  580.9 10.9 %psum.515 = f32[2,128]{1,0:T(2,128)S(1)} all-reduce(f32[2,128]{1,0:T(2,128)S(1)} %broadcast_multiply_fusion.5), channel_id=1, replica_groups=mesh['height_0'=4,'height_1'=2,'plane_0'=2,'plane_1'=4,'plane_2'=4] {'he..., use_global_device_ids=true, to_apply=%region_79.80 | all-reduce | flops 256 | bytes 2048 | tf_op jit(solution)/shard_map/psum | solution.py:31
  599.1 8.8 %psum.518 = f32[2,128]{1,0:T(2,128)S(1)} all-reduce(f32[2,128]{1,0:T(2,128)S(1)} %psum.517), channel_id=1, replica_groups=mesh['height_0'=4,'height_1'=2,'plane_0'=2,'plane_1'=4,'plane_2'=4] {'pl..., use_global_device_ids=true, to_apply=%region_82.83 | all-reduce | flops 256 | bytes 2048 | tf_op jit(solution)/shard_map/psum | solution.py:31
  608.0 10.3 %psum.519 = f32[2,128]{1,0:T(2,128)} all-reduce(f32[2,128]{1,0:T(2,128)S(1)} %psum.518), channel_id=1, replica_groups=mesh['height_0'=4,'height_1'=2,'plane_0'=2,'plane_1'=4,'plane_2'=4] {'pl..., use_global_device_ids=true, to_apply=%region_83.84 | all-reduce | flops 256 | bytes 2048 | tf_op jit(solution)/shard_map/psum | solution.py:31
  (773 shorter events, 303.2 us)
Async XLA Ops:
  3.8 10.8 %collective-permute-start.5 = (f32[1,16,128]{2,1,0:T(8,128)S(1)}, f32[1,16,128]{2,1,0:T(8,128)S(1)}, u32[]{:S(2)}, u32[]{:S(2)}) collective-permute-start(f32[1,16,128]{2,1,0:T(8,128)S(1)} %bitcast.647), channel_id=1, source_target_pairs={{1,0},{2,1},{3,2},{4,3},{5,4},{6,5},{7,6},{8,7},{9,8},{10,9},{11,1... | collective-permute-start | bytes 24584 | tf_op jit(solution)/shard_map/ppermute | solution.py:24
  10.4 7.3 %collective-permute-start.1 = (f32[1,16,128]{2,1,0:T(8,128)S(1)}, f32[1,16,128]{2,1,0:T(8,128)S(1)}, u32[]{:S(2)}, u32[]{:S(2)}) collective-permute-start(f32[1,16,128]{2,1,0:T(8,128)S(1)} %bitcast.645), channel_id=1, source_target_pairs={{1,0},{2,1},{3,2},{4,3},{5,4},{6,5},{7,6},{8,7},{9,8},{10,9},{11,1... | collective-permute-start | bytes 24584 | tf_op jit(solution)/shard_map/ppermute | solution.py:24
  14.6 9.8 %collective-permute-start.4 = (f32[1,16,128]{2,1,0:T(8,128)S(1)}, f32[1,16,128]{2,1,0:T(8,128)S(1)}, u32[]{:S(2)}, u32[]{:S(2)}) collective-permute-start(f32[1,16,128]{2,1,0:T(8,128)S(1)} %bitcast.667), channel_id=1, source_target_pairs={{0,1},{1,2},{2,3},{3,4},{4,5},{5,6},{6,7},{7,8},{8,9},{9,10},{10,1... | collective-permute-start | bytes 24584 | tf_op jit(solution)/shard_map/ppermute | solution.py:21
  17.7 13.2 %collective-permute-start = (f32[1,16,128]{2,1,0:T(8,128)S(1)}, f32[1,16,128]{2,1,0:T(8,128)S(1)}, u32[]{:S(2)}, u32[]{:S(2)}) collective-permute-start(f32[1,16,128]{2,1,0:T(8,128)S(1)} %bitcast.666), channel_id=1, source_target_pairs={{0,1},{1,2},{2,3},{3,4},{4,5},{5,6},{6,7},{7,8},{8,9},{9,10},{10,1... | collective-permute-start | bytes 24584 | tf_op jit(solution)/shard_map/ppermute | solution.py:21
  41.0 14.3 %collective-permute-start.6 = (f32[1,8,128]{2,1,0:T(8,128)S(1)}, f32[1,8,128]{2,1,0:T(8,128)S(1)}, u32[]{:S(2)}, u32[]{:S(2)}) collective-permute-start(f32[1,8,128]{2,1,0:T(8,128)S(1)} %get-tuple-element.205), channel_id=1, source_target_pairs={{0,32},{32,64},{64,96},{96,128},{128,160},{160,192},{192,224},{1,3... | collective-permute-start | bytes 12296 | tf_op jit(solution)/shard_map/ppermute | solution.py:21
  42.4 12.9 %collective-permute-start.7 = (f32[1,8,128]{2,1,0:T(8,128)S(1)}, f32[1,8,128]{2,1,0:T(8,128)S(1)}, u32[]{:S(2)}, u32[]{:S(2)}) collective-permute-start(f32[1,8,128]{2,1,0:T(8,128)S(1)} %get-tuple-element.206), channel_id=1, source_target_pairs={{32,0},{64,32},{96,64},{128,96},{160,128},{192,160},{224,192},{33,... | collective-permute-start | bytes 12296 | tf_op jit(solution)/shard_map/ppermute | solution.py:24
  45.8 9.7 %collective-permute-start.2 = (f32[1,8,128]{2,1,0:T(8,128)S(1)}, f32[1,8,128]{2,1,0:T(8,128)S(1)}, u32[]{:S(2)}, u32[]{:S(2)}) collective-permute-start(f32[1,8,128]{2,1,0:T(8,128)S(1)} %get-tuple-element.211), channel_id=1, source_target_pairs={{0,32},{32,64},{64,96},{96,128},{128,160},{160,192},{192,224},{1,3... | collective-permute-start | bytes 12296 | tf_op jit(solution)/shard_map/ppermute | solution.py:21
  52.4 5.2 collective-permute-start.3
  62.8 5.5 collective-permute-start.9
  68.4 9.8 %collective-permute-start.8 = (f32[1,16,128]{2,1,0:T(8,128)S(1)}, f32[1,16,128]{2,1,0:T(8,128)S(1)}, u32[]{:S(2)}, u32[]{:S(2)}) collective-permute-start(f32[1,16,128]{2,1,0:T(8,128)S(1)} %bitcast.672), channel_id=1, source_target_pairs={{0,1},{1,2},{2,3},{3,4},{4,5},{5,6},{6,7},{7,8},{8,9},{9,10},{10,1... | collective-permute-start | bytes 24584 | tf_op jit(solution)/shard_map/ppermute | solution.py:21
  86.7 5.0 collective-permute-start.10
  89.6 7.4 %collective-permute-start.11 = (f32[1,8,128]{2,1,0:T(8,128)S(1)}, f32[1,8,128]{2,1,0:T(8,128)S(1)}, u32[]{:S(2)}, u32[]{:S(2)}) collective-permute-start(f32[1,8,128]{2,1,0:T(8,128)S(1)} %get-tuple-element.193), channel_id=1, source_target_pairs={{32,0},{64,32},{96,64},{128,96},{160,128},{192,160},{224,192},{33,... | collective-permute-start | bytes 12296 | tf_op jit(solution)/shard_map/ppermute | solution.py:24
  146.8 5.5 collective-permute-start.13
  152.4 10.0 %collective-permute-start.12 = (f32[1,16,128]{2,1,0:T(8,128)S(1)}, f32[1,16,128]{2,1,0:T(8,128)S(1)}, u32[]{:S(2)}, u32[]{:S(2)}) collective-permute-start(f32[1,16,128]{2,1,0:T(8,128)S(1)} %bitcast.674), channel_id=1, source_target_pairs={{0,1},{1,2},{2,3},{3,4},{4,5},{5,6},{6,7},{7,8},{8,9},{9,10},{10,1... | collective-permute-start | bytes 24584 | tf_op jit(solution)/shard_map/ppermute | solution.py:21
  172.3 4.4 collective-permute-start.15
  229.6 5.5 collective-permute-start.17
  235.1 9.8 %collective-permute-start.16 = (f32[1,16,128]{2,1,0:T(8,128)S(1)}, f32[1,16,128]{2,1,0:T(8,128)S(1)}, u32[]{:S(2)}, u32[]{:S(2)}) collective-permute-start(f32[1,16,128]{2,1,0:T(8,128)S(1)} %bitcast.675), channel_id=1, source_target_pairs={{0,1},{1,2},{2,3},{3,4},{4,5},{5,6},{6,7},{7,8},{8,9},{9,10},{10,1... | collective-permute-start | bytes 24584 | tf_op jit(solution)/shard_map/ppermute | solution.py:21
  254.8 4.5 collective-permute-start.19
  307.0 6.0 collective-permute-start.21
  310.9 9.8 %collective-permute-start.20 = (f32[1,16,128]{2,1,0:T(8,128)S(1)}, f32[1,16,128]{2,1,0:T(8,128)S(1)}, u32[]{:S(2)}, u32[]{:S(2)}) collective-permute-start(f32[1,16,128]{2,1,0:T(8,128)S(1)} %bitcast.668), channel_id=1, source_target_pairs={{0,1},{1,2},{2,3},{3,4},{4,5},{5,6},{6,7},{7,8},{8,9},{9,10},{10,1... | collective-permute-start | bytes 24584 | tf_op jit(solution)/shard_map/ppermute | solution.py:21
  330.8 4.4 collective-permute-start.23
  340.5 5.5 collective-permute-start.25
  346.1 9.8 %collective-permute-start.24 = (f32[1,16,128]{2,1,0:T(8,128)S(1)}, f32[1,16,128]{2,1,0:T(8,128)S(1)}, u32[]{:S(2)}, u32[]{:S(2)}) collective-permute-start(f32[1,16,128]{2,1,0:T(8,128)S(1)} %bitcast.676), channel_id=1, source_target_pairs={{0,1},{1,2},{2,3},{3,4},{4,5},{5,6},{6,7},{7,8},{8,9},{9,10},{10,1... | collective-permute-start | bytes 24584 | tf_op jit(solution)/shard_map/ppermute | solution.py:21
  364.4 5.0 collective-permute-start.26
  367.3 4.9 collective-permute-start.27
  421.0 6.1 collective-permute-start.29
  427.2 10.0 %collective-permute-start.28 = (f32[1,16,128]{2,1,0:T(8,128)S(1)}, f32[1,16,128]{2,1,0:T(8,128)S(1)}, u32[]{:S(2)}, u32[]{:S(2)}) collective-permute-start(f32[1,16,128]{2,1,0:T(8,128)S(1)} %bitcast.670), channel_id=1, source_target_pairs={{0,1},{1,2},{2,3},{3,4},{4,5},{5,6},{6,7},{7,8},{8,9},{9,10},{10,1... | collective-permute-start | bytes 24584 | tf_op jit(solution)/shard_map/ppermute | solution.py:21
  445.8 3.5 collective-permute-start.30
  447.1 4.4 collective-permute-start.31
  503.5 5.5 collective-permute-start.33
  509.1 9.8 %collective-permute-start.32 = (f32[1,16,128]{2,1,0:T(8,128)S(1)}, f32[1,16,128]{2,1,0:T(8,128)S(1)}, u32[]{:S(2)}, u32[]{:S(2)}) collective-permute-start(f32[1,16,128]{2,1,0:T(8,128)S(1)} %bitcast.669), channel_id=1, source_target_pairs={{0,1},{1,2},{2,3},{3,4},{4,5},{5,6},{6,7},{7,8},{8,9},{9,10},{10,1... | collective-permute-start | bytes 24584 | tf_op jit(solution)/shard_map/ppermute | solution.py:21
  528.7 4.4 collective-permute-start.35
  (178 other events, 2178.7 us)
where the time goes:
time: 631 us; the launch traced here: 619 us
  blocking collectives  285 us (45%)
  local copies, waits for them, and re-layouts  105 us (17%)
  starting transfers between devices  91.2 us (14%)
  waiting for transfers between devices  87.5 us (14%)
  between operations  24.2 us (4%)
  matrix products  13.4 us (2%)
  other arithmetic  12.3 us (2%)
    psum x35, blocking collectives, by_axis(): value = lax.psum(value, axis)  285 us
    ppermute x18, waiting for transfers between devices, with_halo(): lax.ppermute(lax.slice_in_dim(block, block.shape[dim] - width, None, axis...  53.2 us
    ppermute x18, starting transfers between devices, with_halo(): lax.ppermute(lax.slice_in_dim(block, 0, width, axis=dim), axis, backward)  47 us
    ppermute x18, starting transfers between devices, with_halo(): lax.ppermute(lax.slice_in_dim(block, block.shape[dim] - width, None, axis...  44.2 us
    unnamed x394, local copies, waits for them, and re-layouts  38.5 us
    slice x18, local copies, waits for them, and re-layouts, pair_sum(): lax.slice_in_dim(slot_first, 0, 1, axis=dim_index)  36.3 us
    ppermute x18, waiting for transfers between devices, with_halo(): lax.ppermute(lax.slice_in_dim(block, 0, width, axis=dim), axis, backward)  34.4 us
  transfers between devices with their start and end apart: 36, of which 22 were waited for; matrix products, arithmetic and copies ran while one was open for 3% of the time, Pallas kernels for 0%

commit v1 on v0

--- a/solution.py
+++ b/solution.py
@@ -28,7 +28,7 @@
 
 def by_axis(value, axes):
     for axis in axes:
-        value = lax.psum(value, axis)
+        value = jnp.sum(lax.all_gather(value, axis), axis=0)
     return value
 
 

time: 631 us -> 733 us (1.16)
  local copies, waits for them, and re-layouts: 105 us -> 192 us
  other arithmetic: 12.3 us -> 49.2 us
  blocking collectives: 285 us -> 262 us
    psum x35 -> x0, blocking collectives: 285 us -> none  [by_axis(): value = lax.psum(value, axis)]
    unnamed x0 -> x30, blocking collectives: none -> 229 us
    unnamed x394 -> x527, local copies, waits for them, and re-layouts: 38.5 us -> 125 us
    reduce_sum x0 -> x65, other arithmetic: none -> 37.5 us  [by_axis(): value = jnp.sum(lax.all_gather(value, axis), axis=0)]
    all_gather x0 -> x5, blocking collectives: none -> 33.3 us  [by_axis(): value = jnp.sum(lax.all_gather(value, axis), axis=0)]
  transfers between devices with their start and end apart: 36 -> 36, of which waited for: 22 -> 22; matrix products, arithmetic and copies ran while one was open for 3% -> 2% of each run, Pallas kernels for 0% -> 0%
where the time goes in v1:
time: 733 us; the launch traced here: 720 us
  blocking collectives  262 us (36%)
  local copies, waits for them, and re-layouts  192 us (26%)
  starting transfers between devices  90.6 us (12%)
  waiting for transfers between devices  89 us (12%)
  other arithmetic  49.2 us (7%)
  between operations  24.2 us (3%)
  matrix products  13.4 us (2%)
    unnamed x30, blocking collectives  229 us
    unnamed x527, local copies, waits for them, and re-layouts  125 us
    ppermute x18, waiting for transfers between devices, with_halo(): lax.ppermute(lax.slice_in_dim(block, block.shape[dim] - width, None, axis...  50.9 us
    ppermute x18, starting transfers between devices, with_halo(): lax.ppermute(lax.slice_in_dim(block, 0, width, axis=dim), axis, backward)  46.8 us
    ppermute x18, starting transfers between devices, with_halo(): lax.ppermute(lax.slice_in_dim(block, block.shape[dim] - width, None, axis...  43.8 us
    ppermute x18, waiting for transfers between devices, with_halo(): lax.ppermute(lax.slice_in_dim(block, 0, width, axis=dim), axis, backward)  38.1 us
    reduce_sum x65, other arithmetic, by_axis(): value = jnp.sum(lax.all_gather(value, axis), axis=0)  37.5 us
    slice x18, local copies, waits for them, and re-layouts, pair_sum(): lax.slice_in_dim(slot_first, 0, 1, axis=dim_index)  36.3 us
  transfers between devices with their start and end apart: 36, of which 22 were waited for; matrix products, arithmetic and copies ran while one was open for 2% of the time, Pallas kernels for 0%

profile of v1, /device:TPU:32, one launch (start us, length us, event | category | flops | bytes accessed | tf_op | source)
XLA Modules:
  0.0 720.0 jit_solution(2539663915305863477)
XLA Ops:
  3.8 6.7 collective-permute-start.5
  46.0 6.5 collective-permute-start.2
  91.1 6.1 collective-permute-done.11
  102.1 13.8 %all-reduce.77 = (f32[4]{0:T(128)S(1)}, f32[4]{0:T(128)S(1)}) all-reduce(f32[4]{0:T(128)S(1)} %dynamic-update-slice, f32[4]{0:T(128)S(1)} %dynamic-update-slice.5), channel_id=1, replica_groups=mesh['height_0'=4,'height_1'=2,'plane_0'=2,'plane_1'=4,'plane_2'=4] {'he..., use_global_device_ids=true, to_apply=%add | all-reduce | flops 8 | bytes 64
  138.0 7.7 %all-reduce.71 = (f32[4]{0:T(128)S(1)}, f32[4]{0:T(128)S(1)}) all-reduce(f32[4]{0:T(128)S(1)} %dynamic-update-slice.3, f32[4]{0:T(128)S(1)} %dynamic-update-slice.8), channel_id=1, replica_groups=mesh['height_0'=4,'height_1'=2,'plane_0'=2,'plane_1'=4,'plane_2'=4] {'pl..., use_global_device_ids=true, to_apply=%add.3 | all-reduce | flops 8 | bytes 64
  149.9 9.1 %all-reduce.65 = (f32[4]{0:T(128)S(1)}, f32[4]{0:T(128)S(1)}) all-reduce(f32[4]{0:T(128)S(1)} %dynamic-update-slice.4, f32[4]{0:T(128)S(1)} %dynamic-update-slice.9), channel_id=1, replica_groups=mesh['height_0'=4,'height_1'=2,'plane_0'=2,'plane_1'=4,'plane_2'=4] {'pl..., use_global_device_ids=true, to_apply=%add.4 | all-reduce | flops 8 | bytes 64
  174.3 7.1 collective-permute-done.12
  199.9 13.0 %all-reduce.76 = (f32[4]{0:T(128)S(1)}, f32[4]{0:T(128)S(1)}) all-reduce(f32[4]{0:T(128)S(1)} %dynamic-update-slice.10, f32[4]{0:T(128)S(1)} %dynamic-update-slice.15), channel_id=1, replica_groups=mesh['height_0'=4,'height_1'=2,'plane_0'=2,'plane_1'=4,'plane_2'=4] {'he..., use_global_device_ids=true, to_apply=%add.10 | all-reduce | flops 8 | bytes 64
  224.8 5.1 all-reduce.82
  233.9 7.7 %all-reduce.70 = (f32[4]{0:T(128)S(1)}, f32[4]{0:T(128)S(1)}) all-reduce(f32[4]{0:T(128)S(1)} %dynamic-update-slice.13, f32[4]{0:T(128)S(1)} %dynamic-update-slice.18), channel_id=1, replica_groups=mesh['height_0'=4,'height_1'=2,'plane_0'=2,'plane_1'=4,'plane_2'=4] {'pl..., use_global_device_ids=true, to_apply=%add.13 | all-reduce | flops 8 | bytes 64
  245.8 8.4 %all-reduce.64 = (f32[4]{0:T(128)S(1)}, f32[4]{0:T(128)S(1)}) all-reduce(f32[4]{0:T(128)S(1)} %dynamic-update-slice.14, f32[4]{0:T(128)S(1)} %dynamic-update-slice.19), channel_id=1, replica_groups=mesh['height_0'=4,'height_1'=2,'plane_0'=2,'plane_1'=4,'plane_2'=4] {'pl..., use_global_device_ids=true, to_apply=%add.14 | all-reduce | flops 8 | bytes 64
  273.7 6.7 collective-permute-done.16
  299.1 13.0 %all-reduce.75 = (f32[4]{0:T(128)S(1)}, f32[4]{0:T(128)S(1)}) all-reduce(f32[4]{0:T(128)S(1)} %dynamic-update-slice.20, f32[4]{0:T(128)S(1)} %dynamic-update-slice.25), channel_id=1, replica_groups=mesh['height_0'=4,'height_1'=2,'plane_0'=2,'plane_1'=4,'plane_2'=4] {'he..., use_global_device_ids=true, to_apply=%add.20 | all-reduce | flops 8 | bytes 64
  332.0 8.1 %all-reduce.69 = (f32[4]{0:T(128)S(1)}, f32[4]{0:T(128)S(1)}) all-reduce(f32[4]{0:T(128)S(1)} %dynamic-update-slice.23, f32[4]{0:T(128)S(1)} %dynamic-update-slice.28), channel_id=1, replica_groups=mesh['height_0'=4,'height_1'=2,'plane_0'=2,'plane_1'=4,'plane_2'=4] {'pl..., use_global_device_ids=true, to_apply=%add.23 | all-reduce | flops 8 | bytes 64
  344.2 8.8 %all-reduce.63 = (f32[4]{0:T(128)S(1)}, f32[4]{0:T(128)S(1)}) all-reduce(f32[4]{0:T(128)S(1)} %dynamic-update-slice.24, f32[4]{0:T(128)S(1)} %dynamic-update-slice.29), channel_id=1, replica_groups=mesh['height_0'=4,'height_1'=2,'plane_0'=2,'plane_1'=4,'plane_2'=4] {'pl..., use_global_device_ids=true, to_apply=%add.24 | all-reduce | flops 8 | bytes 64
  365.5 7.6 %collective-permute-done.20 = f32[1,16,128]{2,1,0:T(8,128)S(1)} collective-permute-done((f32[1,16,128]{2,1,0:T(8,128)S(1)}, f32[1,16,128]{2,1,0:T(8,128)S(1)}, u32[]{:S(2)}, u32[]{:S(2)}) %collective-permute-start.20) | collective-permute-done | bytes 8224 | tf_op jit(solution)/shard_map/ppermute | solution.py:21
  400.6 7.6 %collective-permute-done.24 = f32[1,16,128]{2,1,0:T(8,128)S(1)} collective-permute-done((f32[1,16,128]{2,1,0:T(8,128)S(1)}, f32[1,16,128]{2,1,0:T(8,128)S(1)}, u32[]{:S(2)}, u32[]{:S(2)}) %collective-permute-start.24) | collective-permute-done | bytes 8224 | tf_op jit(solution)/shard_map/ppermute | solution.py:21
  428.8 13.2 %all-reduce.74 = (f32[4]{0:T(128)S(1)}, f32[4]{0:T(128)S(1)}) all-reduce(f32[4]{0:T(128)S(1)} %dynamic-update-slice.30, f32[4]{0:T(128)S(1)} %dynamic-update-slice.35), channel_id=1, replica_groups=mesh['height_0'=4,'height_1'=2,'plane_0'=2,'plane_1'=4,'plane_2'=4] {'he..., use_global_device_ids=true, to_apply=%add.30 | all-reduce | flops 8 | bytes 64
  454.6 4.9 all-reduce.80
  463.3 7.7 %all-reduce.68 = (f32[4]{0:T(128)S(1)}, f32[4]{0:T(128)S(1)}) all-reduce(f32[4]{0:T(128)S(1)} %dynamic-update-slice.33, f32[4]{0:T(128)S(1)} %dynamic-update-slice.38), channel_id=1, replica_groups=mesh['height_0'=4,'height_1'=2,'plane_0'=2,'plane_1'=4,'plane_2'=4] {'pl..., use_global_device_ids=true, to_apply=%add.33 | all-reduce | flops 8 | bytes 64
  475.1 7.7 %all-reduce.62 = (f32[4]{0:T(128)S(1)}, f32[4]{0:T(128)S(1)}) all-reduce(f32[4]{0:T(128)S(1)} %dynamic-update-slice.34, f32[4]{0:T(128)S(1)} %dynamic-update-slice.39), channel_id=1, replica_groups=mesh['height_0'=4,'height_1'=2,'plane_0'=2,'plane_1'=4,'plane_2'=4] {'pl..., use_global_device_ids=true, to_apply=%add.34 | all-reduce | flops 8 | bytes 64
  499.7 6.5 collective-permute-done.28
  524.7 13.0 %all-reduce.73 = (f32[4]{0:T(128)S(1)}, f32[4]{0:T(128)S(1)}) all-reduce(f32[4]{0:T(128)S(1)} %dynamic-update-slice.40, f32[4]{0:T(128)S(1)} %dynamic-update-slice.45), channel_id=1, replica_groups=mesh['height_0'=4,'height_1'=2,'plane_0'=2,'plane_1'=4,'plane_2'=4] {'he..., use_global_device_ids=true, to_apply=%add.40 | all-reduce | flops 8 | bytes 64
  558.5 7.7 %all-reduce.67 = (f32[4]{0:T(128)S(1)}, f32[4]{0:T(128)S(1)}) all-reduce(f32[4]{0:T(128)S(1)} %dynamic-update-slice.43, f32[4]{0:T(128)S(1)} %dynamic-update-slice.48), channel_id=1, replica_groups=mesh['height_0'=4,'height_1'=2,'plane_0'=2,'plane_1'=4,'plane_2'=4] {'pl..., use_global_device_ids=true, to_apply=%add.43 | all-reduce | flops 8 | bytes 64
  570.4 8.8 %all-reduce.61 = (f32[4]{0:T(128)S(1)}, f32[4]{0:T(128)S(1)}) all-reduce(f32[4]{0:T(128)S(1)} %dynamic-update-slice.44, f32[4]{0:T(128)S(1)} %dynamic-update-slice.49), channel_id=1, replica_groups=mesh['height_0'=4,'height_1'=2,'plane_0'=2,'plane_1'=4,'plane_2'=4] {'pl..., use_global_device_ids=true, to_apply=%add.44 | all-reduce | flops 8 | bytes 64
  599.1 6.6 collective-permute-done.32
  624.3 13.0 %all-reduce.72 = (f32[4]{0:T(128)S(1)}, f32[4]{0:T(128)S(1)}) all-reduce(f32[4]{0:T(128)S(1)} %dynamic-update-slice.50, f32[4]{0:T(128)S(1)} %dynamic-update-slice.55), channel_id=1, replica_groups=mesh['height_0'=4,'height_1'=2,'plane_0'=2,'plane_1'=4,'plane_2'=4] {'he..., use_global_device_ids=true, to_apply=%add.50 | all-reduce | flops 8 | bytes 64
  657.4 7.7 %all-reduce.66 = (f32[4]{0:T(128)S(1)}, f32[4]{0:T(128)S(1)}) all-reduce(f32[4]{0:T(128)S(1)} %dynamic-update-slice.53, f32[4]{0:T(128)S(1)} %dynamic-update-slice.58), channel_id=1, replica_groups=mesh['height_0'=4,'height_1'=2,'plane_0'=2,'plane_1'=4,'plane_2'=4] {'pl..., use_global_device_ids=true, to_apply=%add.53 | all-reduce | flops 8 | bytes 64
  669.3 8.6 %all-reduce.60 = (f32[4]{0:T(128)S(1)}, f32[4]{0:T(128)S(1)}) all-reduce(f32[4]{0:T(128)S(1)} %dynamic-update-slice.54, f32[4]{0:T(128)S(1)} %dynamic-update-slice.59), channel_id=1, replica_groups=mesh['height_0'=4,'height_1'=2,'plane_0'=2,'plane_1'=4,'plane_2'=4] {'pl..., use_global_device_ids=true, to_apply=%add.54 | all-reduce | flops 8 | bytes 64
  685.0 10.2 %all-gather.5 = f32[4,2,128]{2,1,0:T(2,128)S(1)} all-gather(f32[1,2,128]{2,1,0:T(2,128)S(1)} %multiply_bitcast_fusion), channel_id=2, replica_groups=mesh['height_0'=4,'height_1'=2,'plane_0'=2,'plane_1'=4,'plane_2'=4] {'he..., dimensions={0}, use_global_device_ids=true | all-gather | bytes 5120 | tf_op jit(solution)/shard_map/all_gather | solution.py:31
  701.2 8.1 %all-gather.8 = f32[4,2,128]{2,1,0:T(2,128)S(1)} all-gather(f32[1,2,128]{2,1,0:T(2,128)S(1)} %bitcast.753), channel_id=5, replica_groups=mesh['height_0'=4,'height_1'=2,'plane_0'=2,'plane_1'=4,'plane_2'=4] {'pl..., dimensions={0}, use_global_device_ids=true | all-gather | bytes 5120 | tf_op jit(solution)/shard_map/all_gather | solution.py:31
  709.3 9.0 %all-gather.9 = f32[4,2,128]{2,1,0:T(2,128)S(1)} all-gather(f32[1,2,128]{2,1,0:T(2,128)S(1)} %bitcast.756), channel_id=6, replica_groups=mesh['height_0'=4,'height_1'=2,'plane_0'=2,'plane_1'=4,'plane_2'=4] {'pl..., dimensions={0}, use_global_device_ids=true | all-gather | bytes 5120 | tf_op jit(solution)/shard_map/all_gather | solution.py:31
  (971 shorter events, 419.8 us)
Async XLA Ops:
  3.8 10.8 %collective-permute-start.5 = (f32[1,16,128]{2,1,0:T(8,128)S(1)}, f32[1,16,128]{2,1,0:T(8,128)S(1)}, u32[]{:S(2)}, u32[]{:S(2)}) collective-permute-start(f32[1,16,128]{2,1,0:T(8,128)S(1)} %bitcast.718), channel_id=1, source_target_pairs={{1,0},{2,1},{3,2},{4,3},{5,4},{6,5},{7,6},{8,7},{9,8},{10,9},{11,1... | collective-permute-start | bytes 24584 | tf_op jit(solution)/shard_map/ppermute | solution.py:24
  10.4 7.3 %collective-permute-start.1 = (f32[1,16,128]{2,1,0:T(8,128)S(1)}, f32[1,16,128]{2,1,0:T(8,128)S(1)}, u32[]{:S(2)}, u32[]{:S(2)}) collective-permute-start(f32[1,16,128]{2,1,0:T(8,128)S(1)} %bitcast.716), channel_id=1, source_target_pairs={{1,0},{2,1},{3,2},{4,3},{5,4},{6,5},{7,6},{8,7},{9,8},{10,9},{11,1... | collective-permute-start | bytes 24584 | tf_op jit(solution)/shard_map/ppermute | solution.py:24
  14.6 9.8 %collective-permute-start.4 = (f32[1,16,128]{2,1,0:T(8,128)S(1)}, f32[1,16,128]{2,1,0:T(8,128)S(1)}, u32[]{:S(2)}, u32[]{:S(2)}) collective-permute-start(f32[1,16,128]{2,1,0:T(8,128)S(1)} %bitcast.739), channel_id=1, source_target_pairs={{0,1},{1,2},{2,3},{3,4},{4,5},{5,6},{6,7},{7,8},{8,9},{9,10},{10,1... | collective-permute-start | bytes 24584 | tf_op jit(solution)/shard_map/ppermute | solution.py:21
  17.8 13.2 %collective-permute-start = (f32[1,16,128]{2,1,0:T(8,128)S(1)}, f32[1,16,128]{2,1,0:T(8,128)S(1)}, u32[]{:S(2)}, u32[]{:S(2)}) collective-permute-start(f32[1,16,128]{2,1,0:T(8,128)S(1)} %bitcast.737), channel_id=1, source_target_pairs={{0,1},{1,2},{2,3},{3,4},{4,5},{5,6},{6,7},{7,8},{8,9},{9,10},{10,1... | collective-permute-start | bytes 24584 | tf_op jit(solution)/shard_map/ppermute | solution.py:21
  41.0 14.5 %collective-permute-start.6 = (f32[1,8,128]{2,1,0:T(8,128)S(1)}, f32[1,8,128]{2,1,0:T(8,128)S(1)}, u32[]{:S(2)}, u32[]{:S(2)}) collective-permute-start(f32[1,8,128]{2,1,0:T(8,128)S(1)} %get-tuple-element.205), channel_id=1, source_target_pairs={{0,32},{32,64},{64,96},{96,128},{128,160},{160,192},{192,224},{1,3... | collective-permute-start | bytes 12296 | tf_op jit(solution)/shard_map/ppermute | solution.py:21
  42.4 13.0 %collective-permute-start.7 = (f32[1,8,128]{2,1,0:T(8,128)S(1)}, f32[1,8,128]{2,1,0:T(8,128)S(1)}, u32[]{:S(2)}, u32[]{:S(2)}) collective-permute-start(f32[1,8,128]{2,1,0:T(8,128)S(1)} %get-tuple-element.206), channel_id=1, source_target_pairs={{32,0},{64,32},{96,64},{128,96},{160,128},{192,160},{224,192},{33,... | collective-permute-start | bytes 12296 | tf_op jit(solution)/shard_map/ppermute | solution.py:24
  46.0 9.7 %collective-permute-start.2 = (f32[1,8,128]{2,1,0:T(8,128)S(1)}, f32[1,8,128]{2,1,0:T(8,128)S(1)}, u32[]{:S(2)}, u32[]{:S(2)}) collective-permute-start(f32[1,8,128]{2,1,0:T(8,128)S(1)} %get-tuple-element.211), channel_id=1, source_target_pairs={{0,32},{32,64},{64,96},{96,128},{128,160},{160,192},{192,224},{1,3... | collective-permute-start | bytes 12296 | tf_op jit(solution)/shard_map/ppermute | solution.py:21
  52.6 5.2 collective-permute-start.3
  63.0 5.5 collective-permute-start.9
  68.6 9.8 %collective-permute-start.8 = (f32[1,16,128]{2,1,0:T(8,128)S(1)}, f32[1,16,128]{2,1,0:T(8,128)S(1)}, u32[]{:S(2)}, u32[]{:S(2)}) collective-permute-start(f32[1,16,128]{2,1,0:T(8,128)S(1)} %bitcast.738), channel_id=1, source_target_pairs={{0,1},{1,2},{2,3},{3,4},{4,5},{5,6},{6,7},{7,8},{8,9},{9,10},{10,1... | collective-permute-start | bytes 24584 | tf_op jit(solution)/shard_map/ppermute | solution.py:21
  86.9 4.2 collective-permute-start.10
  89.8 7.4 %collective-permute-start.11 = (f32[1,8,128]{2,1,0:T(8,128)S(1)}, f32[1,8,128]{2,1,0:T(8,128)S(1)}, u32[]{:S(2)}, u32[]{:S(2)}) collective-permute-start(f32[1,8,128]{2,1,0:T(8,128)S(1)} %get-tuple-element.193), channel_id=1, source_target_pairs={{32,0},{64,32},{96,64},{128,96},{160,128},{192,160},{224,192},{33,... | collective-permute-start | bytes 12296 | tf_op jit(solution)/shard_map/ppermute | solution.py:24
  166.1 5.5 collective-permute-start.13
  171.6 9.8 %collective-permute-start.12 = (f32[1,16,128]{2,1,0:T(8,128)S(1)}, f32[1,16,128]{2,1,0:T(8,128)S(1)}, u32[]{:S(2)}, u32[]{:S(2)}) collective-permute-start(f32[1,16,128]{2,1,0:T(8,128)S(1)} %bitcast.743), channel_id=1, source_target_pairs={{0,1},{1,2},{2,3},{3,4},{4,5},{5,6},{6,7},{7,8},{8,9},{9,10},{10,1... | collective-permute-start | bytes 24584 | tf_op jit(solution)/shard_map/ppermute | solution.py:21
  191.3 4.4 collective-permute-start.15
  264.9 5.5 collective-permute-start.17
  270.4 10.0 %collective-permute-start.16 = (f32[1,16,128]{2,1,0:T(8,128)S(1)}, f32[1,16,128]{2,1,0:T(8,128)S(1)}, u32[]{:S(2)}, u32[]{:S(2)}) collective-permute-start(f32[1,16,128]{2,1,0:T(8,128)S(1)} %bitcast.744), channel_id=1, source_target_pairs={{0,1},{1,2},{2,3},{3,4},{4,5},{5,6},{6,7},{7,8},{8,9},{9,10},{10,1... | collective-permute-start | bytes 24584 | tf_op jit(solution)/shard_map/ppermute | solution.py:21
  290.3 4.5 collective-permute-start.19
  359.6 5.9 collective-permute-start.21
  363.3 9.8 %collective-permute-start.20 = (f32[1,16,128]{2,1,0:T(8,128)S(1)}, f32[1,16,128]{2,1,0:T(8,128)S(1)}, u32[]{:S(2)}, u32[]{:S(2)}) collective-permute-start(f32[1,16,128]{2,1,0:T(8,128)S(1)} %bitcast.740), channel_id=1, source_target_pairs={{0,1},{1,2},{2,3},{3,4},{4,5},{5,6},{6,7},{7,8},{8,9},{9,10},{10,1... | collective-permute-start | bytes 24584 | tf_op jit(solution)/shard_map/ppermute | solution.py:21
  381.9 3.4 collective-permute-start.22
  383.2 4.4 collective-permute-start.23
  392.9 5.5 collective-permute-start.25
  398.5 9.8 %collective-permute-start.24 = (f32[1,16,128]{2,1,0:T(8,128)S(1)}, f32[1,16,128]{2,1,0:T(8,128)S(1)}, u32[]{:S(2)}, u32[]{:S(2)}) collective-permute-start(f32[1,16,128]{2,1,0:T(8,128)S(1)} %bitcast.745), channel_id=1, source_target_pairs={{0,1},{1,2},{2,3},{3,4},{4,5},{5,6},{6,7},{7,8},{8,9},{9,10},{10,1... | collective-permute-start | bytes 24584 | tf_op jit(solution)/shard_map/ppermute | solution.py:21
  416.8 4.2 collective-permute-start.26
  419.7 4.9 collective-permute-start.27
  490.0 6.1 collective-permute-start.29
  496.2 10.0 %collective-permute-start.28 = (f32[1,16,128]{2,1,0:T(8,128)S(1)}, f32[1,16,128]{2,1,0:T(8,128)S(1)}, u32[]{:S(2)}, u32[]{:S(2)}) collective-permute-start(f32[1,16,128]{2,1,0:T(8,128)S(1)} %bitcast.746), channel_id=1, source_target_pairs={{0,1},{1,2},{2,3},{3,4},{4,5},{5,6},{6,7},{7,8},{8,9},{9,10},{10,1... | collective-permute-start | bytes 24584 | tf_op jit(solution)/shard_map/ppermute | solution.py:21
  516.1 4.4 collective-permute-start.31
  590.4 5.5 collective-permute-start.33
  595.9 9.8 %collective-permute-start.32 = (f32[1,16,128]{2,1,0:T(8,128)S(1)}, f32[1,16,128]{2,1,0:T(8,128)S(1)}, u32[]{:S(2)}, u32[]{:S(2)}) collective-permute-start(f32[1,16,128]{2,1,0:T(8,128)S(1)} %bitcast.741), channel_id=1, source_target_pairs={{0,1},{1,2},{2,3},{3,4},{4,5},{5,6},{6,7},{7,8},{8,9},{9,10},{10,1... | collective-permute-start | bytes 24584 | tf_op jit(solution)/shard_map/ppermute | solution.py:21
  615.6 4.4 collective-permute-start.35
  (182 other events, 1732.4 us)
